TPU v7x, 512 devices: a whole 4x8x8 slice. The times are simulated.
512 devices in a mesh: section: 4 (over x), frame: 16 (over y_lo, z), chan: 8 (over y_hi, core).
Axes of the slice: x: 4, y: 8 (y_hi: 4, y_lo: 2; y = y_hi * 2 + y_lo), z: 8, core: 2. Of those that a mesh axis runs over, the one named last changes fastest.
Arguments:
- upstream: bfloat16 [512, 8, 16, 128], P('chan', None, 'frame'), may hold values from -6 to 6
- acts: bfloat16 [4, 512, 8, 16, 128], P('section', None, None, 'frame'), may hold values from -6 to 6
- weights: bfloat16 [4, 27, 512, 512], P('section', None, 'chan'), may hold values from -0.0625 to 0.0625
Outputs:
- grads: bfloat16 [4, 512, 8, 16, 128], P('section', 'chan', None, 'frame')
- weight_grads: bfloat16 [4, 27, 512, 512], P('section', None, 'chan')
All inputs are finite; a program needn't handle non-finite values.
Results may differ from a plain program's by a relative error of at most 0.03.
Values may be sent and summed in bfloat16 or wider, within the bound.
A program may use at most 64 MiB of HBM per device.

v0:
```python
import jax
import jax.numpy as jnp
from jax import lax
from jax.sharding import PartitionSpec as P

BLOCK_FRAMES = 2


def with_halo(cells, sides, width):
    for axis, dim in sides:
        count = lax.axis_size(axis)
        ends = count - 1
        head = lax.slice_in_dim(cells, 0, width, axis=dim)
        tail = lax.slice_in_dim(cells, cells.shape[dim] - width, cells.shape[dim], axis=dim)
        cells = jnp.concatenate(
            [
                lax.ppermute(tail, axis, [(i, (i + 1) % count) for i in range(ends)]),
                cells,
                lax.ppermute(head, axis, [((i + 1) % count, i) for i in range(ends)]),
            ],
            axis=dim,
        )
    return cells


def shifted(value, axis, steps):
    count = lax.axis_size(axis)
    leading, last = (max(0, -steps), min(count, count - steps))
    return lax.ppermute(value, axis, [(source, source + steps) for source in range(leading, last)])


def derivative(stored):
    logistic = jax.nn.sigmoid(stored)
    return logistic * (1.0 + stored * (1.0 - logistic))


def tap_matrix(extended, frames_n, rows_n, width_n):
    pieces = []
    for t_lag in range(3):
        for r_off in (-1, 0, 1):
            for w_off in (-1, 0, 1):
                pieces.append(
                    extended[
                        :,
                        t_lag : t_lag + frames_n,
                        1 - r_off : 1 - r_off + rows_n,
                        1 - w_off : 1 - w_off + width_n,
                    ]
                )
    stacked = jnp.stack(pieces, axis=0)
    return stacked.reshape(stacked.shape[0] * stacked.shape[1], -1)


def body(upstream, acts, weights):
    group = upstream.shape[0]
    frames_all = upstream.shape[1]
    rows_n = upstream.shape[2]
    width_n = upstream.shape[3]
    channels = acts.shape[1]
    blocks_n = frames_all // BLOCK_FRAMES
    cells = BLOCK_FRAMES * rows_n * width_n
    sections = lax.axis_size("section")
    section_pos = lax.axis_index("section")
    chan_pos = lax.axis_index("chan")
    kernel_mat = weights[0].reshape(27 * group, channels)
    stored_all = acts[0]
    later = jnp.zeros((group, 2, rows_n + 2, width_n), jnp.bfloat16)
    inbound = jnp.zeros((group, BLOCK_FRAMES, rows_n, width_n), jnp.bfloat16)
    results = jnp.zeros((group, frames_all, rows_n, width_n), jnp.bfloat16)
    kernel_sum = jnp.zeros((27 * group, channels), jnp.float32)
    ticks = blocks_n + sections - 1
    for tick in range(ticks):
        order = tick - section_pos
        active = jnp.logical_and(order >= 0, order < blocks_n)
        first = (blocks_n - 1 - jnp.clip(order, 0, blocks_n - 1)) * BLOCK_FRAMES
        fresh = lax.dynamic_slice_in_dim(upstream, first, BLOCK_FRAMES, 1)
        current = jnp.where(section_pos == 0, fresh, inbound)
        framed = with_halo(current, (("frame", 2),), 1)
        extended = jnp.pad(
            jnp.concatenate([framed, later], axis=1), ((0, 0), (0, 0), (0, 0), (1, 1))
        )
        taps_mat = tap_matrix(extended, BLOCK_FRAMES, rows_n, width_n)
        stored = lax.dynamic_slice_in_dim(stored_all, first, BLOCK_FRAMES, 1)

        def busy(operand):
            return lax.dot_general(
                kernel_mat, taps_mat, (((0,), (0,)), ((), ())), preferred_element_type=jnp.float32
            )

        def resting(operand):
            return jnp.zeros((group * lax.axis_size("chan"), cells), jnp.float32)

        summed = lax.psum_scatter(
            lax.cond(active, busy, resting, 0).astype(jnp.bfloat16),
            "chan",
            scatter_dimension=0,
            tiled=True,
        ).astype(jnp.float32)
        own = lax.dynamic_slice_in_dim(stored, chan_pos * group, group, 0).astype(jnp.float32)
        updated = (
            current.astype(jnp.float32) + derivative(own) * summed.reshape(current.shape)
        ).astype(jnp.bfloat16)

        def add_kernel(total):
            values = stored.astype(jnp.float32)
            features = (
                (values * jax.nn.sigmoid(values)).astype(jnp.bfloat16).reshape(channels, cells)
            )
            return total + lax.dot_general(
                taps_mat, features, (((1,), (1,)), ((), ())), preferred_element_type=jnp.float32
            )

        def keep_kernel(total):
            return total

        kernel_sum = lax.cond(active, add_kernel, keep_kernel, kernel_sum)
        written = lax.dynamic_update_slice_in_dim(results, updated, first, 1)
        results = jnp.where(active, written, results)
        later = jnp.where(active, framed, later)
        if tick + 1 < ticks:
            inbound = shifted(updated, "section", 1)
    kernel_total = lax.psum(kernel_sum.astype(jnp.bfloat16), "frame")
    return (results[None], kernel_total.reshape(1, 27, group, channels))


def solution(mesh):
    placed = (
        P("chan", None, "frame", None),
        P("section", None, None, "frame", None),
        P("section", None, "chan", None),
    )
    return jax.shard_map(
        body,
        mesh=mesh,
        in_specs=placed,
        out_specs=(P("section", "chan", None, "frame", None), P("section", None, "chan", None)),
        check_vma=False,
    )
```

profile of v0, /device:TPU:2, one launch (start us, length us, event | category | flops | bytes accessed | tf_op | source)
XLA Modules:
  0.0 595.2 jit_solution(7948391413461682318)
XLA Ops:
  8.2 4.3 collective-permute-start
  14.0 4.6 collective-permute-done.1
  23.6 43.8 %reduce-scatter.8.cloned.1.call-done = bf16[64,256]{1,0:T(8,128)(2,1)} async-done(((bf16[512,256]{1,0:T(8,128)(2,1)}), bf16[64,256]{1,0:T(8,128)(2,1)}) %reduce-scatter.8.cloned.1.call-update) | async-done | bytes 32784 | tf_op jit(solution)/shard_map/reduce_scatter | solution.py:93
  68.4 3.4 collective-permute-start.2
  71.8 2.4 collective-permute-done.2
  74.3 3.5 collective-permute-start.3
  79.4 4.2 collective-permute-done.4
  88.0 2.4 conditional.15
  88.0 2.4 fusion.222
  91.2 36.6 %reduce-scatter.10.cloned.1.call-done = bf16[64,256]{1,0:T(8,128)(2,1)} async-done(((bf16[512,256]{1,0:T(8,128)(2,1)}), bf16[64,256]{1,0:T(8,128)(2,1)}) %reduce-scatter.10.cloned.1.call-update) | async-done | bytes 32784 | tf_op jit(solution)/shard_map/reduce_scatter | solution.py:93
  128.8 3.3 collective-permute-start.5
  132.2 2.4 collective-permute-done.5
  134.7 3.5 collective-permute-start.6
  139.8 4.2 collective-permute-done.7
  148.1 2.4 conditional.16
  148.1 2.4 fusion.223
  151.3 38.1 %reduce-scatter.12.cloned.1.call-done = bf16[64,256]{1,0:T(8,128)(2,1)} async-done(((bf16[512,256]{1,0:T(8,128)(2,1)}), bf16[64,256]{1,0:T(8,128)(2,1)}) %reduce-scatter.12.cloned.1.call-update) | async-done | bytes 32784 | tf_op jit(solution)/shard_map/reduce_scatter | solution.py:93
  190.5 3.3 collective-permute-start.8
  193.8 2.5 collective-permute-done.8
  197.6 4.7 collective-permute-start.9
  208.2 2.4 conditional.17
  211.4 39.8 %reduce-scatter.14.cloned.1.call-done = bf16[64,256]{1,0:T(8,128)(2,1)} async-done(((bf16[512,256]{1,0:T(8,128)(2,1)}), bf16[64,256]{1,0:T(8,128)(2,1)}) %reduce-scatter.14.cloned.1.call-update) | async-done | bytes 32784 | tf_op jit(solution)/shard_map/reduce_scatter | solution.py:93
  252.2 3.4 collective-permute-start.11
  258.1 3.6 collective-permute-start.12
  263.2 4.2 collective-permute-done.13
  271.5 2.4 conditional.18
  271.5 2.4 fusion.225
  274.7 38.2 %reduce-scatter.16.cloned.1.call-done = bf16[64,256]{1,0:T(8,128)(2,1)} async-done(((bf16[512,256]{1,0:T(8,128)(2,1)}), bf16[64,256]{1,0:T(8,128)(2,1)}) %reduce-scatter.16.cloned.1.call-update) | async-done | bytes 32784 | tf_op jit(solution)/shard_map/reduce_scatter | solution.py:93
  313.9 3.3 collective-permute-start.14
  317.2 2.5 collective-permute-done.14
  319.8 3.6 collective-permute-start.15
  325.0 4.2 collective-permute-done.16
  334.4 40.5 %reduce-scatter.18.cloned.1.call-done = bf16[64,256]{1,0:T(8,128)(2,1)} async-done(((bf16[512,256]{1,0:T(8,128)(2,1)}), bf16[64,256]{1,0:T(8,128)(2,1)}) %reduce-scatter.18.cloned.1.call-update) | async-done | bytes 32784 | tf_op jit(solution)/shard_map/reduce_scatter | solution.py:93
  375.9 3.4 collective-permute-start.17
  379.2 2.4 collective-permute-done.17
  381.8 3.5 collective-permute-start.18
  386.9 4.2 collective-permute-done.19
  396.4 6.4 %conditional.22 = (f32[1728,512]{1,0:T(8,128)S(1)}) conditional(s32[]{:T(128)} %convert_element_type.269, f32[1728,512]{1,0:T(8,128)S(1)} %get-tuple-element.296, (bf16[1,512,8,1,128]{4,2,3,1,0:T(8,128)(2,1)}, bf16[1728,256]{1,0:T(8,128)(2,1)}, f32[1728,512]{1,0:T(8,128)S(1)}, s32[]{:T(128)}) %tuple.125), branch_computations={%region_23.24_spmd, %region_24.25_spmd.clone} | conditional | flops 454656000 | bytes 11894796 | solution.py:116
  396.4 3.4 copy.28
  402.8 6.8 %conditional.23 = (f32[1728,512]{1,0:T(8,128)S(1)}) conditional(s32[]{:T(128)} %convert_element_type.275, f32[1728,512]{1,0:T(8,128)S(1)} %get-tuple-element.297, (bf16[1,512,8,1,128]{4,2,3,1,0:T(8,128)(2,1)}, bf16[1728,256]{1,0:T(8,128)(2,1)}, f32[1728,512]{1,0:T(8,128)S(1)}, s32[]{:T(128)}) %tuple.126), branch_computations={%region_25.26_spmd, %region_26.27_spmd.clone} | conditional | flops 454656000 | bytes 11894796 | solution.py:116
  403.2 3.4 copy.29
  409.6 6.4 %conditional.24 = (f32[1728,512]{1,0:T(8,128)S(1)}) conditional(s32[]{:T(128)} %convert_element_type.281, f32[1728,512]{1,0:T(8,128)S(1)} %get-tuple-element.298, (bf16[1,512,8,1,128]{4,2,3,1,0:T(8,128)(2,1)}, bf16[1728,256]{1,0:T(8,128)(2,1)}, f32[1728,512]{1,0:T(8,128)S(1)}, s32[]{:T(128)}) %tuple.127), branch_computations={%region_27.28_spmd, %region_28.29_spmd.clone} | conditional | flops 454656000 | bytes 11894796 | solution.py:116
  409.6 3.4 copy.30
  416.0 6.6 %conditional.25 = (f32[1728,512]{1,0:T(8,128)S(1)}) conditional(s32[]{:T(128)} %convert_element_type.287, f32[1728,512]{1,0:T(8,128)S(1)} %get-tuple-element.299, (bf16[1,512,8,1,128]{4,2,3,1,0:T(8,128)(2,1)}, bf16[1728,256]{1,0:T(8,128)(2,1)}, f32[1728,512]{1,0:T(8,128)S(1)}, s32[]{:T(128)}) %tuple.128), branch_computations={%region_29.30_spmd, %region_30.31_spmd.clone} | conditional | flops 454656000 | bytes 11894796 | solution.py:116
  416.2 3.4 copy.31
  425.2 10.9 %reduce-scatter.20.cloned.1.call-done = bf16[64,256]{1,0:T(8,128)(2,1)} async-done(((bf16[512,256]{1,0:T(8,128)(2,1)}), bf16[64,256]{1,0:T(8,128)(2,1)}) %reduce-scatter.20.cloned.1.call-update) | async-done | bytes 32784 | tf_op jit(solution)/shard_map/reduce_scatter | solution.py:93
  438.1 147.1 %all-reduce.10.cloned.1.call-done = bf16[1,27,64,512]{3,2,1,0:T(8,128)(2,1)} async-done(((bf16[1,27,64,512]{3,2,1,0:T(8,128)(2,1)}), bf16[1,27,64,512]{3,2,1,0:T(8,128)(2,1)}) %all-reduce.10.cloned.1.call-update) | async-done | bytes 1769488 | tf_op jit(solution)/shard_map/psum | solution.py:122
  585.3 2.9 copy.307
  (312 shorter events, 76.2 us)
Async XLA Ops:
  7.2 60.2 %reduce-scatter.8.cloned.1.call-start = ((), (), s32[]{:S(2)}) async-start(), calls=%async_computation.7 | async-start | bytes 294912 | tf_op jit(solution)/shard_map/reduce_scatter | solution.py:93
  8.2 5.9 collective-permute-start
  12.5 6.2 %collective-permute-start.1 = (bf16[64,2,1,128]{3,1,0,2:T(2,128)(2,1)S(1)}, bf16[64,2,1,128]{3,1,0,2:T(2,128)(2,1)S(1)}, u32[]{:S(2)}, u32[]{:S(2)}) collective-permute-start(bf16[64,2,1,128]{3,1,0,2:T(2,128)(2,1)S(1)} %broadcast_select_fusion.18), channel_id=1, source_target_pairs={{8,0},{16,8},{24,16},{32,24},{40,32},{48,40},{56,48},{64,56},{72,6... | collective-permute-start | bytes 98312 | tf_op jit(solution)/shard_map/ppermute | solution.py:19
  22.7 45.5 %copy-start = (bf16[1,512,8,1,128]{4,2,3,1,0:T(8,128)(2,1)S(1)}, bf16[1,512,8,1,128]{4,2,3,1,0:T(8,128)(2,1)}, u32[]{:S(2)}) copy-start(bf16[1,512,8,1,128]{4,2,3,1,0:T(8,128)(2,1)} %param.32) | copy-start | bytes 3145732
  22.7 45.5 %copy-start.10 = (bf16[64,8,1,128]{3,1,2,0:T(8,128)(2,1)S(1)}, bf16[64,8,1,128]{3,1,2,0:T(8,128)(2,1)}, u32[]{:S(2)}) copy-start(bf16[64,8,1,128]{3,1,2,0:T(8,128)(2,1)} %param.31) | copy-start | bytes 393220
  22.8 0.7 copy-start.3
  23.5 104.3 %reduce-scatter.10.cloned.1.call-start = ((), (), s32[]{:S(2)}) async-start(), calls=%async_computation.8 | async-start | bytes 294912 | tf_op jit(solution)/shard_map/reduce_scatter | solution.py:93
  68.4 5.8 collective-permute-start.2
  74.3 5.1 collective-permute-start.3
  77.9 5.8 collective-permute-start.4
  90.5 0.7 copy-start.4
  91.2 98.2 %reduce-scatter.12.cloned.1.call-start = ((), (), s32[]{:S(2)}) async-start(), calls=%async_computation.9 | async-start | bytes 294912 | tf_op jit(solution)/shard_map/reduce_scatter | solution.py:93
  128.8 5.8 collective-permute-start.5
  134.7 5.1 collective-permute-start.6
  138.2 5.8 collective-permute-start.7
  150.5 0.7 copy-start.5
  151.3 99.9 %reduce-scatter.14.cloned.1.call-start = ((), (), s32[]{:S(2)}) async-start(), calls=%async_computation.10 | async-start | bytes 294912 | tf_op jit(solution)/shard_map/reduce_scatter | solution.py:93
  190.5 5.8 collective-permute-start.8
  196.3 6.0 %collective-permute-start.10 = (bf16[64,2,1,128]{3,1,0,2:T(2,128)(2,1)S(1)}, bf16[64,2,1,128]{3,1,0,2:T(2,128)(2,1)S(1)}, u32[]{:S(2)}, u32[]{:S(2)}) collective-permute-start(bf16[64,2,1,128]{3,1,0,2:T(2,128)(2,1)S(1)} %broadcast_select_fusion.15), channel_id=1, source_target_pairs={{8,0},{16,8},{24,16},{32,24},{40,32},{48,40},{56,48},{64,56},{72,6... | collective-permute-start | bytes 98312 | tf_op jit(solution)/shard_map/ppermute | solution.py:19
  197.6 6.1 %collective-permute-start.9 = (bf16[64,2,1,128]{3,1,0,2:T(2,128)(2,1)S(1)}, bf16[64,2,1,128]{3,1,0,2:T(2,128)(2,1)S(1)}, u32[]{:S(2)}, u32[]{:S(2)}) collective-permute-start(bf16[64,2,1,128]{3,1,0,2:T(2,128)(2,1)S(1)} %broadcast_select_fusion.15), channel_id=1, source_target_pairs={{0,8},{8,16},{16,24},{24,32},{32,40},{40,48},{48,56},{56,64},{64,7... | collective-permute-start | bytes 98312 | tf_op jit(solution)/shard_map/ppermute | solution.py:17
  210.6 0.7 copy-start.6
  211.3 101.6 %reduce-scatter.16.cloned.1.call-start = ((), (), s32[]{:S(2)}) async-start(), calls=%async_computation.11 | async-start | bytes 294912 | tf_op jit(solution)/shard_map/reduce_scatter | solution.py:93
  252.2 5.8 collective-permute-start.11
  258.1 5.2 collective-permute-start.12
  261.7 5.8 collective-permute-start.13
  273.9 0.7 copy-start.7
  274.6 100.2 %reduce-scatter.18.cloned.1.call-start = ((), (), s32[]{:S(2)}) async-start(), calls=%async_computation.12 | async-start | bytes 294912 | tf_op jit(solution)/shard_map/reduce_scatter | solution.py:93
  313.9 5.8 collective-permute-start.14
  319.8 5.2 collective-permute-start.15
  323.4 5.8 collective-permute-start.16
  333.6 0.7 copy-start.8
  334.3 101.8 %reduce-scatter.20.cloned.1.call-start = ((), (), s32[]{:S(2)}) async-start(), calls=%async_computation.13 | async-start | bytes 294912 | tf_op jit(solution)/shard_map/reduce_scatter | solution.py:93
  375.9 20.1 %copy-start.2 = (bf16[64,8,1,128]{3,1,0,2:T(8,128)(2,1)}, bf16[64,8,1,128]{3,1,0,2:T(8,128)(2,1)S(1)}, u32[]{:S(2)}) copy-start(bf16[64,8,1,128]{3,1,0,2:T(8,128)(2,1)S(1)} %get-tuple-element.271) | copy-start | bytes 393220
  375.9 5.8 collective-permute-start.17
  381.7 11.8 %copy-start.11 = (bf16[64,2,1,128]{3,1,0,2:T(2,128)(2,1)}, bf16[64,2,1,128]{3,1,0,2:T(2,128)(2,1)S(1)}, u32[]{:S(2)}) copy-start(bf16[64,2,1,128]{3,1,0,2:T(2,128)(2,1)S(1)} %broadcast_select_fusion.12) | copy-start | bytes 98308
  381.8 5.1 collective-permute-start.18
  385.3 5.8 collective-permute-start.19
  395.2 0.7 copy-start.9
  395.9 189.4 %all-reduce.10.cloned.1.call-start = ((), (), s32[]{:S(2)}) async-start(), calls=%async_computation.14 | async-start | bytes 3538944 | tf_op jit(solution)/shard_map/psum | solution.py:122
  424.3 12.6 %copy-start.12 = (bf16[64,2,1,128]{3,1,0,2:T(2,128)(2,1)S(1)}, bf16[64,2,1,128]{3,1,0,2:T(2,128)(2,1)}, u32[]{:S(2)}) copy-start(bf16[64,2,1,128]{3,1,0,2:T(2,128)(2,1)} %copy-done.11) | copy-start | bytes 98308
  438.1 150.0 %copy-start.13 = (bf16[1,64,8,1,128]{4,2,3,1,0:T(8,128)(2,1)}, bf16[1,64,8,1,128]{4,2,3,1,0:T(8,128)(2,1)S(1)}, u32[]{:S(2)}) copy-start(bf16[1,64,8,1,128]{4,2,3,1,0:T(8,128)(2,1)S(1)} %fusion.88) | copy-start | bytes 393220
Sparse Core Ops, SparseCore 0:
  23.7 43.6 reduce-scatter.7
  91.3 36.4 reduce-scatter.9
  151.4 38.0 reduce-scatter.11
  211.4 39.6 reduce-scatter.13
  274.7 38.1 reduce-scatter.15
  334.5 40.3 reduce-scatter.17
  396.0 40.0 reduce-scatter.19
  439.9 145.2 all-reduce.9
where the time goes:
time: 605 us; the launch traced here: 595 us
  waiting for transfers between devices  438 us (72%)
  starting transfers between devices  56.5 us (9%)
  local copies, waits for them, and re-layouts  54 us (9%)
  matrix products  17.1 us (3%)
  between operations  15.3 us (3%)
  other arithmetic  13.1 us (2%)
    reduce_scatter x7, waiting for transfers between devices, body(): lax.psum_scatter(lax.cond(active, busy, resting, 0).astype(jnp.bfloat16),...  248 us
    psum x1, waiting for transfers between devices, body(): kernel_total = lax.psum(kernel_sum.astype(jnp.bfloat16), 'frame')  147 us
    unnamed x216, local copies, waits for them, and re-layouts  33.3 us
    ppermute x7, starting transfers between devices, with_halo(): lax.ppermute(tail, axis, [(i, (i + 1) % count) for i in range(ends)])  26.8 us
    ppermute x7, waiting for transfers between devices, with_halo(): lax.ppermute(head, axis, [((i + 1) % count, i) for i in range(ends)])  25.7 us
    ppermute x6, starting transfers between devices, shifted(): lax.ppermute(value, axis, [(source, source + steps) for source in range(l...  20.1 us
    ppermute x6, waiting for transfers between devices, shifted(): lax.ppermute(value, axis, [(source, source + steps) for source in range(l...  14.6 us
    another operation x7, local copies, waits for them, and re-layouts  13.6 us
  transfers between devices with their start and end apart: 28, of which 27 were waited for; matrix products, arithmetic and copies ran while one was open for 5% of the time, Pallas kernels for 0%

commit v1 on v0

--- a/solution.py
+++ b/solution.py
@@ -119,7 +119,7 @@
         later = jnp.where(active, framed, later)
         if tick + 1 < ticks:
             inbound = shifted(updated, "section", 1)
-    kernel_total = lax.psum(kernel_sum.astype(jnp.bfloat16), "frame")
+    kernel_total = jnp.sum(lax.all_gather(kernel_sum.astype(jnp.bfloat16), "frame"), axis=0)
     return (results[None], kernel_total.reshape(1, 27, group, channels))
 
 

time: 605 us -> 771 us (1.27)
  the two profiles are of different devices: /device:TPU:2 before, /device:TPU:1 now
where the time goes in v1:
time: 771 us; the launch traced here: 761 us
  waiting for transfers between devices  591 us (77%)
  starting transfers between devices  57.7 us (7%)
  local copies, waits for them, and re-layouts  49.5 us (6%)
  other arithmetic  24.7 us (3%)
  matrix products  16.9 us (2%)
  between operations  15.3 us (2%)
    all_gather x1, waiting for transfers between devices, body(): lax.all_gather(kernel_sum.astype(jnp.bfloat16), 'frame')  305 us
    reduce_scatter x7, waiting for transfers between devices, body(): lax.psum_scatter(lax.cond(active, busy, resting, 0).astype(jnp.bfloat16),...  273 us
    unnamed x215, local copies, waits for them, and re-layouts  30.5 us
    ppermute x7, starting transfers between devices, with_halo(): lax.ppermute(tail, axis, [(i, (i + 1) % count) for i in range(ends)])  29.8 us
    ppermute x6, starting transfers between devices, shifted(): lax.ppermute(value, axis, [(source, source + steps) for source in range(l...  18.5 us
  transfers between devices with their start and end apart: 28, of which 21 were waited for; matrix products, arithmetic and copies ran while one was open for 4% of the time, Pallas kernels for 0%

profile of v1, /device:TPU:1, one launch (start us, length us, event | category | flops | bytes accessed | tf_op | source)
XLA Modules:
  0.0 761.0 jit_solution(8189631263631125123)
XLA Ops:
  8.2 1.3 collective-permute-start.1
  9.5 5.5 collective-permute-start
  20.1 2.3 conditional.14
  20.1 2.3 fusion.221
  23.1 43.9 %reduce-scatter.8.cloned.1.call-done = bf16[64,256]{1,0:T(8,128)(2,1)} async-done(((bf16[512,256]{1,0:T(8,128)(2,1)}), bf16[64,256]{1,0:T(8,128)(2,1)}) %reduce-scatter.8.cloned.1.call-update) | async-done | bytes 32784 | tf_op jit(solution)/shard_map/reduce_scatter | solution.py:93
  68.1 3.1 collective-permute-start.2
  72.2 1.3 collective-permute-start.4
  73.5 4.0 collective-permute-start.3
  82.9 2.4 conditional.15
  82.9 2.4 fusion.222
  86.0 41.3 %reduce-scatter.10.cloned.1.call-done = bf16[64,256]{1,0:T(8,128)(2,1)} async-done(((bf16[512,256]{1,0:T(8,128)(2,1)}), bf16[64,256]{1,0:T(8,128)(2,1)}) %reduce-scatter.10.cloned.1.call-update) | async-done | bytes 32784 | tf_op jit(solution)/shard_map/reduce_scatter | solution.py:93
  128.3 3.1 collective-permute-start.5
  132.5 1.3 collective-permute-start.7
  133.8 4.0 collective-permute-start.6
  142.9 2.4 conditional.16
  142.9 2.4 fusion.223
  146.1 42.8 %reduce-scatter.12.cloned.1.call-done = bf16[64,256]{1,0:T(8,128)(2,1)} async-done(((bf16[512,256]{1,0:T(8,128)(2,1)}), bf16[64,256]{1,0:T(8,128)(2,1)}) %reduce-scatter.12.cloned.1.call-update) | async-done | bytes 32784 | tf_op jit(solution)/shard_map/reduce_scatter | solution.py:93
  189.9 3.0 collective-permute-start.8
  194.0 1.3 collective-permute-start.10
  195.3 4.2 collective-permute-start.9
  204.7 2.4 conditional.17
  204.7 2.4 fusion.224
  207.9 42.7 %reduce-scatter.14.cloned.1.call-done = bf16[64,256]{1,0:T(8,128)(2,1)} async-done(((bf16[512,256]{1,0:T(8,128)(2,1)}), bf16[64,256]{1,0:T(8,128)(2,1)}) %reduce-scatter.14.cloned.1.call-update) | async-done | bytes 32784 | tf_op jit(solution)/shard_map/reduce_scatter | solution.py:93
  251.6 3.1 collective-permute-start.11
  257.1 4.1 collective-permute-start.12
  267.0 45.0 %reduce-scatter.16.cloned.1.call-done = bf16[64,256]{1,0:T(8,128)(2,1)} async-done(((bf16[512,256]{1,0:T(8,128)(2,1)}), bf16[64,256]{1,0:T(8,128)(2,1)}) %reduce-scatter.16.cloned.1.call-update) | async-done | bytes 32784 | tf_op jit(solution)/shard_map/reduce_scatter | solution.py:93
  313.0 3.1 collective-permute-start.14
  318.4 4.0 collective-permute-start.15
  328.6 45.0 %reduce-scatter.18.cloned.1.call-done = bf16[64,256]{1,0:T(8,128)(2,1)} async-done(((bf16[512,256]{1,0:T(8,128)(2,1)}), bf16[64,256]{1,0:T(8,128)(2,1)}) %reduce-scatter.18.cloned.1.call-update) | async-done | bytes 32784 | tf_op jit(solution)/shard_map/reduce_scatter | solution.py:93
  374.7 3.1 collective-permute-start.17
  380.2 4.2 collective-permute-start.18
  390.0 5.1 conditional.21
  390.1 2.2 copy.27
  393.4 1.8 convolution_bitcast_fusion
  395.2 6.4 conditional.22
  395.2 3.4 copy.28
  399.7 1.9 bitcast_add_fusion
  401.6 6.8 conditional.23
  402.0 3.4 copy.29
  406.5 1.9 bitcast_add_fusion.1
  408.4 6.4 conditional.24
  408.4 3.4 copy.30
  412.9 1.9 bitcast_add_fusion.2
  415.0 5.0 conditional.27
  420.1 1.4 convert_element_type.304
  422.4 12.4 %reduce-scatter.20.cloned.1.call-done = bf16[64,256]{1,0:T(8,128)(2,1)} async-done(((bf16[512,256]{1,0:T(8,128)(2,1)}), bf16[64,256]{1,0:T(8,128)(2,1)}) %reduce-scatter.20.cloned.1.call-update) | async-done | bytes 32784 | tf_op jit(solution)/shard_map/reduce_scatter | solution.py:93
  436.9 305.4 %all-gather.3.cloned.1.call-done = bf16[27648,512]{1,0:T(8,128)(2,1)} async-done(((bf16[1728,512]{1,0:T(8,128)(2,1)}), bf16[27648,512]{1,0:T(8,128)(2,1)}) %all-gather.3.cloned.1.call-update) | async-done | bytes 28311568 | tf_op jit(solution)/shard_map/all_gather | solution.py:122
  742.3 11.6 %reduce_sum.12 = bf16[1728,512]{1,0:T(8,128)(2,1)} reduce(bf16[16,1728,512]{2,1,0:T(8,128)(2,1)} %bitcast.902, bf16[]{:T(256)} %constant.234.clone.1), dimensions={0}, to_apply=%region_35.36 | reduce | flops 13271040 | bytes 30081026 | tf_op jit(solution)/shard_map/reduce_sum | solution.py:122
  (313 shorter events, 65.9 us)
Async XLA Ops:
  7.2 59.8 %reduce-scatter.8.cloned.1.call-start = ((), (), s32[]{:S(2)}) async-start(), calls=%async_computation.7 | async-start | bytes 294912 | tf_op jit(solution)/shard_map/reduce_scatter | solution.py:93
  8.2 6.8 collective-permute-start.1
  9.5 6.5 collective-permute-start
  20.0 47.8 %copy-start = (bf16[1,512,8,1,128]{4,2,3,1,0:T(8,128)(2,1)S(1)}, bf16[1,512,8,1,128]{4,2,3,1,0:T(8,128)(2,1)}, u32[]{:S(2)}) copy-start(bf16[1,512,8,1,128]{4,2,3,1,0:T(8,128)(2,1)} %param.32) | copy-start | bytes 3145732
  20.1 47.8 %copy-start.10 = (bf16[64,8,1,128]{3,1,2,0:T(8,128)(2,1)S(1)}, bf16[64,8,1,128]{3,1,2,0:T(8,128)(2,1)}, u32[]{:S(2)}) copy-start(bf16[64,8,1,128]{3,1,2,0:T(8,128)(2,1)} %param.31) | copy-start | bytes 393220
  22.3 0.7 copy-start.3
  23.1 104.2 %reduce-scatter.10.cloned.1.call-start = ((), (), s32[]{:S(2)}) async-start(), calls=%async_computation.8 | async-start | bytes 294912 | tf_op jit(solution)/shard_map/reduce_scatter | solution.py:93
  68.1 4.1 collective-permute-start.2
  72.2 5.3 collective-permute-start.4
  73.5 5.0 collective-permute-start.3
  85.3 0.7 copy-start.4
  86.0 102.9 %reduce-scatter.12.cloned.1.call-start = ((), (), s32[]{:S(2)}) async-start(), calls=%async_computation.9 | async-start | bytes 294912 | tf_op jit(solution)/shard_map/reduce_scatter | solution.py:93
  128.3 4.1 collective-permute-start.5
  132.5 5.3 collective-permute-start.7
  133.8 5.0 collective-permute-start.6
  145.3 0.7 copy-start.5
  146.0 104.6 %reduce-scatter.14.cloned.1.call-start = ((), (), s32[]{:S(2)}) async-start(), calls=%async_computation.10 | async-start | bytes 294912 | tf_op jit(solution)/shard_map/reduce_scatter | solution.py:93
  189.9 4.0 collective-permute-start.8
  194.0 5.5 collective-permute-start.10
  195.3 5.0 collective-permute-start.9
  207.1 0.7 copy-start.6
  207.8 104.1 %reduce-scatter.16.cloned.1.call-start = ((), (), s32[]{:S(2)}) async-start(), calls=%async_computation.11 | async-start | bytes 294912 | tf_op jit(solution)/shard_map/reduce_scatter | solution.py:93
  251.6 4.1 collective-permute-start.11
  255.8 5.4 collective-permute-start.13
  257.1 5.1 collective-permute-start.12
  266.2 0.7 copy-start.7
  266.9 106.7 %reduce-scatter.18.cloned.1.call-start = ((), (), s32[]{:S(2)}) async-start(), calls=%async_computation.12 | async-start | bytes 294912 | tf_op jit(solution)/shard_map/reduce_scatter | solution.py:93
  313.0 4.1 collective-permute-start.14
  317.1 5.3 collective-permute-start.16
  318.4 5.0 collective-permute-start.15
  327.8 0.7 copy-start.8
  328.6 106.3 %reduce-scatter.20.cloned.1.call-start = ((), (), s32[]{:S(2)}) async-start(), calls=%async_computation.13 | async-start | bytes 294912 | tf_op jit(solution)/shard_map/reduce_scatter | solution.py:93
  374.7 15.4 %copy-start.2 = (bf16[64,8,1,128]{3,1,0,2:T(8,128)(2,1)}, bf16[64,8,1,128]{3,1,0,2:T(8,128)(2,1)S(1)}, u32[]{:S(2)}) copy-start(bf16[64,8,1,128]{3,1,0,2:T(8,128)(2,1)S(1)} %get-tuple-element.271) | copy-start | bytes 393220
  374.7 4.1 collective-permute-start.17
  378.9 8.8 %copy-start.11 = (bf16[64,2,1,128]{3,1,0,2:T(2,128)(2,1)}, bf16[64,2,1,128]{3,1,0,2:T(2,128)(2,1)S(1)}, u32[]{:S(2)}) copy-start(bf16[64,2,1,128]{3,1,0,2:T(2,128)(2,1)S(1)} %broadcast_select_fusion.12) | copy-start | bytes 98308
  378.9 5.5 collective-permute-start.19
  380.2 5.0 collective-permute-start.18
  389.2 0.7 copy-start.9
  390.0 352.3 %all-gather.3.cloned.1.call-start = ((), (), s32[]{:S(2)}) async-start(), calls=%async_computation.14 | async-start | bytes 30081024 | tf_op jit(solution)/shard_map/all_gather | solution.py:122
  390.1 3.3 copy-start.1
  421.5 14.2 %copy-start.12 = (bf16[64,2,1,128]{3,1,0,2:T(2,128)(2,1)S(1)}, bf16[64,2,1,128]{3,1,0,2:T(2,128)(2,1)}, u32[]{:S(2)}) copy-start(bf16[64,2,1,128]{3,1,0,2:T(2,128)(2,1)} %copy-done.11) | copy-start | bytes 98308
  436.9 317.0 %copy-start.13 = (bf16[1,64,8,1,128]{4,2,3,1,0:T(8,128)(2,1)}, bf16[1,64,8,1,128]{4,2,3,1,0:T(8,128)(2,1)S(1)}, u32[]{:S(2)}) copy-start(bf16[1,64,8,1,128]{4,2,3,1,0:T(8,128)(2,1)S(1)} %fusion.88) | copy-start | bytes 393220
Sparse Core Ops, SparseCore 0:
  23.2 43.7 reduce-scatter.7
  86.1 41.1 reduce-scatter.9
  146.1 42.6 reduce-scatter.11
  208.0 42.5 reduce-scatter.13
  267.1 44.8 reduce-scatter.15
  328.7 44.9 reduce-scatter.17
  390.1 44.7 reduce-scatter.19
  437.7 304.5 all-gather.2
